TPU v7x, 32 devices: a whole 2x2x4 slice. The times are simulated.
32 devices in a mesh: vblk: 8 (over y, x, core), pair: 4 (over z).
Axes of the slice: x: 2, y: 2, z: 4, core: 2. Of those that a mesh axis runs over, the one named last changes fastest.
Arguments:
- amplitudes: bfloat16 [128, 384, 384], P(('vblk', 'pair')), may hold values from -6 to 6
- domain_mask: int32 [128, 3], P(('vblk', 'pair')), may hold values from 0 to 1, as said below
- centers: int32 [128], P(('vblk', 'pair')), may hold values from 0 to 7, as said below
- chol_panel: bfloat16 [8, 8, 5, 128, 128], P('vblk', None, None, 'pair'), may hold values from -0.3125 to 0.3125
Outputs:
- residual_tiles: float32 [128, 384, 384], P(('vblk', 'pair'))
Inputs may be any that keep to these rules, and one draw needn't show every extreme that they name: centers[p] differs from p // 16 (the block of the region that holds pair p) by at most 1, and by exactly 1 in both directions for some pairs. `domain_mask`: the middle column of the window (column 1 for a window of 3 blocks) is 1 for every pair; column k is 0 where the window block centers + k minus the middle index lies outside 0 to 7.
All inputs are finite; a program needn't handle non-finite values.
Results may differ from a plain program's by a relative error of at most 0.0029.
Values may be sent and summed in bfloat16 or wider, within the bound.
No kernel may reach another device: no remote copies, remote signals or barrier semaphores. Data moves between devices by JAX's collectives and lax.ppermute only.
A program may use at most 128 MiB of HBM per device.

v0:
```python
import jax
import jax.numpy as jnp
from jax import lax
from jax.sharding import PartitionSpec as P

VB = 128
DW = 3
RCH = 1


def from_behind(value, axis, steps):
    count = lax.axis_size(axis)
    first, last = (max(0, -steps), min(count, count - steps))
    return lax.ppermute(value, axis, [(source, source + steps) for source in range(first, last)])


def assemble(window):
    strips = []
    for a in range(DW):
        strips.append(
            jnp.concatenate([window[..., a, :, b - a + DW - 1, :, :] for b in range(DW)], axis=-1)
        )
    return jnp.concatenate(strips, axis=-2)


def local(amplitudes, domain_mask, centers, chol_panel):
    halfwidth = (DW - 1) // 2
    furthest = RCH + halfwidth
    whole = lax.all_gather(chol_panel, "pair", axis=3, tiled=True)
    nearby = []
    for distance in range(-furthest, furthest + 1):
        if distance == 0:
            nearby.append(whole)
        else:
            nearby.append(from_behind(whole, "vblk", -distance))
    neighbourhood = jnp.concatenate(nearby, axis=0)
    position = lax.axis_index("vblk")
    offset = centers - position + furthest - halfwidth
    row_index = offset[:, None] + jnp.arange(DW, dtype=jnp.int32)[None, :]
    window = jnp.take(neighbourhood, row_index, axis=0)
    blocks = assemble(window)
    live_cols = jnp.repeat(domain_mask, VB, axis=1) > 0
    keep_tile = live_cols[:, :, None] & live_cols[:, None, :]
    masked = jnp.where(keep_tile, amplitudes, jnp.zeros_like(amplitudes))
    half_product = jnp.einsum(
        "pqij,pjk->pqik", blocks, masked, preferred_element_type=jnp.float32
    ).astype(jnp.bfloat16)
    ladder = jnp.einsum("pqik,pqlk->pil", half_product, blocks, preferred_element_type=jnp.float32)
    return jnp.where(keep_tile, ladder, jnp.zeros_like(ladder))


def solution(mesh):
    return jax.shard_map(
        local,
        mesh=mesh,
        in_specs=(
            P(("vblk", "pair"), None, None),
            P(("vblk", "pair"), None),
            P(("vblk", "pair")),
            P("vblk", None, None, "pair", None),
        ),
        out_specs=P(("vblk", "pair"), None, None),
        check_vma=False,
    )
```

profile of v0, /device:TPU:0, one launch (start us, length us, event | category | flops | bytes accessed | tf_op | source)
XLA Modules:
  0.0 181.5 jit_solution(7642532700543118598)
XLA Ops:
  6.5 0.0 all-gather.2.cloned.1.call-start
  6.5 0.7 all-gather.2.cloned.1.call-update
  7.3 37.1 %all-gather.2.cloned.1.call-done = bf16[1,8,5,128,128]{4,3,2,1,0:T(8,128)(2,1)} async-done(((bf16[1,8,5,32,128]{4,3,2,1,0:T(8,128)(2,1)}), bf16[1,8,5,128,128]{4,3,2,1,0:T(8,128)(2,1)}) %all-gather.2.cloned.1.call-update) | async-done | bytes 1310736 | tf_op jit(solution)/shard_map/all_gather | solution.py:29
  44.4 3.4 %collective-permute-start = (bf16[1,8,5,128,128]{4,3,2,1,0:T(8,128)(2,1)}, bf16[1,8,5,128,128]{4,3,2,1,0:T(8,128)(2,1)S(1)}, u32[]{:S(2)}, u32[]{:S(2)}) collective-permute-start(bf16[1,8,5,128,128]{4,3,2,1,0:T(8,128)(2,1)} %all-gather.2.cloned.1.call-done), channel_id=1, source_target_pairs={{0,8},{4,12},{8,16},{12,20},{16,24},{20,28},{1,9},{5,13},{9,17},{1... | collective-permute-start | bytes 3932168 | tf_op jit(solution)/shard_map/ppermute | solution.py:14
  47.8 2.4 %collective-permute-start.1 = (bf16[1,8,5,128,128]{4,3,2,1,0:T(8,128)(2,1)}, bf16[1,8,5,128,128]{4,3,2,1,0:T(8,128)(2,1)}, u32[]{:S(2)}, u32[]{:S(2)}) collective-permute-start(bf16[1,8,5,128,128]{4,3,2,1,0:T(8,128)(2,1)} %all-gather.2.cloned.1.call-done), channel_id=1, source_target_pairs={{0,4},{4,8},{8,12},{12,16},{16,20},{20,24},{24,28},{1,5},{5,9},{9,... | collective-permute-start | bytes 3932168 | tf_op jit(solution)/shard_map/ppermute | solution.py:14
  50.2 0.7 subtract_add_fusion
  50.8 1.3 collective-permute-start.2
  52.1 0.1 compare_select_fusion
  52.2 0.1 reshape.71
  52.3 1.3 collective-permute-start.3
  53.6 0.1 fusion.17
  53.6 0.1 copy.7
  53.8 0.7 broadcast_compare_fusion
  54.4 0.1 copy.6
  54.6 0.1 broadcast_bitcast_fusion
  54.6 22.6 %collective-permute-done = bf16[1,8,5,128,128]{4,3,2,1,0:T(8,128)(2,1)S(1)} collective-permute-done((bf16[1,8,5,128,128]{4,3,2,1,0:T(8,128)(2,1)}, bf16[1,8,5,128,128]{4,3,2,1,0:T(8,128)(2,1)S(1)}, u32[]{:S(2)}, u32[]{:S(2)}) %collective-permute-start) | collective-permute-done | bytes 1310752 | tf_op jit(solution)/shard_map/ppermute | solution.py:14
  77.3 1.2 constant_dynamic-update-slice_fusion.4
  78.4 0.0 collective-permute-done.1
  78.4 2.5 %constant_dynamic-update-slice_fusion.3 = bf16[5,8,5,128,128]{4,3,2,1,0:T(8,128)(2,1)} fusion(bf16[5,8,5,128,128]{4,3,2,1,0:T(8,128)(2,1)} %constant_dynamic-update-slice_fusion.4, bf16[1,8,5,128,128]{4,3,2,1,0:T(8,128)(2,1)} %collective-permute-done.1), kind=kLoop, calls=%fused_computation.24 | loop fusion | bytes 2621440
  81.0 2.5 %constant_dynamic-update-slice_fusion.2 = bf16[5,8,5,128,128]{4,3,2,1,0:T(8,128)(2,1)} fusion(bf16[5,8,5,128,128]{4,3,2,1,0:T(8,128)(2,1)} %constant_dynamic-update-slice_fusion.3, bf16[1,8,5,128,128]{4,3,2,1,0:T(8,128)(2,1)} %all-gather.2.cloned.1.call-done), kind=kLoop, calls=%fused_computation.23 | loop fusion | bytes 2621440
  83.5 0.0 collective-permute-done.2
  83.5 1.1 constant_dynamic-update-slice_fusion.1
  84.6 48.8 %collective-permute-done.3 = bf16[1,8,5,128,128]{4,3,2,1,0:T(8,128)(2,1)} collective-permute-done((bf16[1,8,5,128,128]{4,3,2,1,0:T(8,128)(2,1)}, bf16[1,8,5,128,128]{4,3,2,1,0:T(8,128)(2,1)}, u32[]{:S(2)}, u32[]{:S(2)}) %collective-permute-start.3) | collective-permute-done | bytes 1310752 | tf_op jit(solution)/shard_map/ppermute | solution.py:14
  133.5 2.6 %constant_dynamic-update-slice_fusion = bf16[5,8,5,128,128]{4,3,2,1,0:T(8,128)(2,1)} fusion(bf16[5,8,5,128,128]{4,3,2,1,0:T(8,128)(2,1)} %constant_dynamic-update-slice_fusion.1, bf16[1,8,5,128,128]{4,3,2,1,0:T(8,128)(2,1)} %collective-permute-done.3), kind=kLoop, calls=%fused_computation.21 | loop fusion | bytes 2621440 | tf_op jit(solution)/shard_map/concatenate | solution.py:36
  136.0 10.0 %gather_fusion = bf16[12,8,5,128,128]{4,3,2,1,0:T(8,128)(2,1)} fusion(bf16[5,8,5,128,128]{4,3,2,1,0:T(8,128)(2,1)} %constant_dynamic-update-slice_fusion, s32[1024]{0:T(1024)S(1)} %pad_clamp_fusion), kind=kCustom, calls=%fused_computation | custom fusion | bytes 31457328 | tf_op jit(solution)/shard_map/jit(_take)/gather | solution.py:40
  146.0 8.3 %copy_select_fusion = bf16[4,3,8,5,128,128]{5,4,2,0,3,1:T(8,128)(2,1)S(1)} fusion(bf16[4,3,8,5,128,128]{5,4,3,2,1,0:T(8,128)(2,1)} %bitcast.39, pred[4,3]{0,1:T(4,128)(4,1)S(1)} %copy.7), kind=kLoop, calls=%fused_computation.1 | loop fusion | flops 7864320 | bytes 31457292 | tf_op jit(solution)/shard_map/jit(_take)/select_n | solution.py:40
  154.3 0.0 copy-start
  154.3 3.3 %slice_bitcast_fusion.8 = (bf16[4,8,128,128]{3,2,1,0:T(8,128)(2,1)S(1)}, bf16[4,8,128,128]{3,2,1,0:T(8,128)(2,1)S(1)}, bf16[4,8,128,128]{3,2,1,0:T(8,128)(2,1)S(...) fusion(bf16[4,3,8,5,128,128]{5,4,2,0,3,1:T(8,128)(2,1)S(1)} %co, ...), kind=kLoop, calls=%fused_computation.19 | loop fusion | bytes 18874368 | tf_op jit(solution)/shard_map/squeeze | solution.py:21
  157.7 0.0 copy-done
  157.7 8.3 %fusion.29 = bf16[4,8,384,384]{3,2,1,0:T(8,128)(2,1)} fusion(bf16[4,8,128,128]{3,2,1,0:T(8,128)(2,1)S(1)} %get-tuple-element.6, bf16[4,8,128,128]{3,2,1,0:T(8,128)(2,1)S(1)} %get-tuple-element.7, bf16[4,8,128,128]{3,2,1,0:T(8,128)(2,1)S(1)} %get-tuple-element.8, bf16[4,8,128,128]{3,2,1,0:T(8,128)(2,1)S(1)} %get-tuple-element.9, ...), kind=kOutput, calls=%fused_computation.4.clone.clone.clone.2 | convolution fusion | flops 3714711552 | bytes 20055552 | tf_op jit(solution)/shard_map/pqij,pjk->pqik/dot_general | solution.py:45
  165.9 8.7 %and_select_fusion = f32[4,384,384]{2,1,0:T(8,128)} fusion(bf16[4,8,128,128]{3,2,1,0:T(8,128)(2,1)S(1)} %get-tuple-element.6, bf16[4,8,128,128]{3,2,1,0:T(8,128)(2,1)S(1)} %get-tuple-element.7, bf16[4,8,128,128]{3,2,1,0:T(8,128)(2,1)S(1)} %get-tuple-element.8, bf16[4,8,128,128]{3,2,1,0:T(8,128)(2,1)S(1)} %get-tuple-element.9, ...), kind=kOutput, calls=%fused_computation.6 | convolution fusion | flops 3709992960 | bytes 21235200 | tf_op jit(solution)/shard_map/pqik,pqlk->pil/dot_general | solution.py:48
  (1 shorter events, 0.0 us)
Async XLA Ops:
  6.5 37.8 %all-gather.2.cloned.1.call-start = ((), (), s32[]{:S(2)}) async-start(), calls=%async_computation | async-start | bytes 1638400 | tf_op jit(solution)/shard_map/all_gather | solution.py:29
  44.4 32.9 %collective-permute-start = (bf16[1,8,5,128,128]{4,3,2,1,0:T(8,128)(2,1)}, bf16[1,8,5,128,128]{4,3,2,1,0:T(8,128)(2,1)S(1)}, u32[]{:S(2)}, u32[]{:S(2)}) collective-permute-start(bf16[1,8,5,128,128]{4,3,2,1,0:T(8,128)(2,1)} %all-gather.2.cloned.1.call-done), channel_id=1, source_target_pairs={{0,8},{4,12},{8,16},{12,20},{16,24},{20,28},{1,9},{5,13},{9,17},{1... | collective-permute-start | bytes 3932168 | tf_op jit(solution)/shard_map/ppermute | solution.py:14
  47.8 30.6 %collective-permute-start.1 = (bf16[1,8,5,128,128]{4,3,2,1,0:T(8,128)(2,1)}, bf16[1,8,5,128,128]{4,3,2,1,0:T(8,128)(2,1)}, u32[]{:S(2)}, u32[]{:S(2)}) collective-permute-start(bf16[1,8,5,128,128]{4,3,2,1,0:T(8,128)(2,1)} %all-gather.2.cloned.1.call-done), channel_id=1, source_target_pairs={{0,4},{4,8},{8,12},{12,16},{16,20},{20,24},{24,28},{1,5},{5,9},{9,... | collective-permute-start | bytes 3932168 | tf_op jit(solution)/shard_map/ppermute | solution.py:14
  50.8 32.6 %collective-permute-start.2 = (bf16[1,8,5,128,128]{4,3,2,1,0:T(8,128)(2,1)}, bf16[1,8,5,128,128]{4,3,2,1,0:T(8,128)(2,1)S(1)}, u32[]{:S(2)}, u32[]{:S(2)}) collective-permute-start(bf16[1,8,5,128,128]{4,3,2,1,0:T(8,128)(2,1)} %all-gather.2.cloned.1.call-done), channel_id=1, source_target_pairs={{4,0},{8,4},{12,8},{16,12},{20,16},{24,20},{28,24},{5,1},{9,5},{13... | collective-permute-start | bytes 3932168 | tf_op jit(solution)/shard_map/ppermute | solution.py:14
  52.3 81.2 %collective-permute-start.3 = (bf16[1,8,5,128,128]{4,3,2,1,0:T(8,128)(2,1)}, bf16[1,8,5,128,128]{4,3,2,1,0:T(8,128)(2,1)}, u32[]{:S(2)}, u32[]{:S(2)}) collective-permute-start(bf16[1,8,5,128,128]{4,3,2,1,0:T(8,128)(2,1)} %all-gather.2.cloned.1.call-done), channel_id=1, source_target_pairs={{8,0},{12,4},{16,8},{20,12},{24,16},{28,20},{9,1},{13,5},{17,9},{2... | collective-permute-start | bytes 3932168 | tf_op jit(solution)/shard_map/ppermute | solution.py:14
  154.3 3.4 %copy-start = (bf16[4,384,384]{2,1,0:T(8,128)(2,1)S(1)}, bf16[4,384,384]{2,1,0:T(8,128)(2,1)}, u32[]{:S(2)}) copy-start(bf16[4,384,384]{2,1,0:T(8,128)(2,1)} %param.4) | copy-start | bytes 3538948
Sparse Core Ops, SparseCore 0:
  8.9 35.3 all-gather.1
where the time goes:
time: 182 us
  waiting for transfers between devices  109 us (60%)
  local copies, waits for them, and re-layouts  23.7 us (13%)
  matrix products  17 us (9%)
  between operations  13.5 us (7%)
  other arithmetic  9.76 us (5%)
  starting transfers between devices  8.37 us (5%)
    ppermute x4, waiting for transfers between devices, from_behind(): lax.ppermute(value, axis, [(source, source + steps) for source in range(f...  71.4 us
    all_gather x1, waiting for transfers between devices, local(): whole = lax.all_gather(chol_panel, 'pair', axis=3, tiled=True)  37.1 us
    gather x1, local copies, waits for them, and re-layouts, local(): window = jnp.take(neighbourhood, row_index, axis=0)  10 us
    dot_general x1, matrix products, local(): jnp.einsum('pqik,pqlk->pil', half_product, blocks, preferred_element_type...  8.71 us
    ppermute x4, starting transfers between devices, from_behind(): lax.ppermute(value, axis, [(source, source + steps) for source in range(f...  8.37 us
    select_n x2, other arithmetic, local(): window = jnp.take(neighbourhood, row_index, axis=0)  8.33 us
    dot_general x1, matrix products, local(): jnp.einsum('pqij,pjk->pqik', blocks, masked, preferred_element_type=jnp.f...  8.28 us
    unnamed x6, local copies, waits for them, and re-layouts  7.38 us
  transfers between devices with their start and end apart: 5, of which 3 were waited for; matrix products, arithmetic and copies ran while one was open for 5% of the time, Pallas kernels for 0%

commit v1 on v0

--- a/solution.py
+++ b/solution.py
@@ -26,7 +26,26 @@
 def local(amplitudes, domain_mask, centers, chol_panel):
     halfwidth = (DW - 1) // 2
     furthest = RCH + halfwidth
-    whole = lax.all_gather(chol_panel, "pair", axis=3, tiled=True)
+    size, index, rows = (lax.axis_size("pair"), lax.axis_index("pair"), chol_panel.shape[3])
+    upward = [(i, (i + 1) % size) for i in range(size)]
+    backward = [(i, (i - 1) % size) for i in range(size)]
+    whole_2 = jnp.zeros(
+        (*chol_panel.shape[:3], size * rows, *chol_panel.shape[3 + 1 :]), chol_panel.dtype
+    )
+    whole_2 = lax.dynamic_update_slice_in_dim(whole_2, chol_panel, index * rows, axis=3)
+    from_left = from_right = chol_panel
+    half = size // 2
+    for step in range(1, half + 1):
+        from_left = lax.ppermute(from_left, "pair", upward)
+        whole_2 = lax.dynamic_update_slice_in_dim(
+            whole_2, from_left, (index - step) % size * rows, axis=3
+        )
+        if step < size - half:
+            from_right = lax.ppermute(from_right, "pair", backward)
+            whole_2 = lax.dynamic_update_slice_in_dim(
+                whole_2, from_right, (index + step) % size * rows, axis=3
+            )
+    whole = whole_2
     nearby = []
     for distance in range(-furthest, furthest + 1):
         if distance == 0:

time: 182 us -> 157 us (0.86)
  waiting for transfers between devices: 109 us -> 90.5 us
  between operations: 13.5 us -> 0.11 us
  starting transfers between devices: 8.37 us -> 13.5 us
    all_gather x1 -> x0, waiting for transfers between devices: 37.1 us -> none  [local(): whole = lax.all_gather(chol_panel, 'pair', axis=3, tiled=True)]
    ppermute x0 -> x3, waiting for transfers between devices: none -> 20.6 us  [the longest x2 16.1 us: local(): from_left = lax.ppermute(from_left, 'pair', upward)]
    ppermute x0 -> x3, starting transfers between devices: none -> 5.05 us  [the longest x2 3.03 us: local(): from_left = lax.ppermute(from_left, 'pair', upward)]
  transfers between devices with their start and end apart: 5 -> 7, of which waited for: 3 -> 5; matrix products, arithmetic and copies ran while one was open for 5% -> 7% of each run, Pallas kernels for 0% -> 0%
where the time goes in v1:
time: 157 us; the launch traced here: 156 us
  waiting for transfers between devices  90.5 us (58%)
  local copies, waits for them, and re-layouts  25.5 us (16%)
  matrix products  17 us (11%)
  starting transfers between devices  13.5 us (9%)
  other arithmetic  9.76 us (6%)
    ppermute x4, waiting for transfers between devices, from_behind(): lax.ppermute(value, axis, [(source, source + steps) for source in range(f...  69.9 us
    ppermute x2, waiting for transfers between devices, local(): from_left = lax.ppermute(from_left, 'pair', upward)  16.1 us
    gather x1, local copies, waits for them, and re-layouts, local(): window = jnp.take(neighbourhood, row_index, axis=0)  10 us
    dot_general x1, matrix products, local(): jnp.einsum('pqik,pqlk->pil', half_product, blocks, preferred_element_type...  8.71 us
    ppermute x4, starting transfers between devices, from_behind(): lax.ppermute(value, axis, [(source, source + steps) for source in range(f...  8.41 us
    select_n x2, other arithmetic, local(): window = jnp.take(neighbourhood, row_index, axis=0)  8.33 us
    dot_general x1, matrix products, local(): jnp.einsum('pqij,pjk->pqik', blocks, masked, preferred_element_type=jnp.f...  8.28 us
    unnamed x6, local copies, waits for them, and re-layouts  7.37 us
  transfers between devices with their start and end apart: 7, of which 5 were waited for; matrix products, arithmetic and copies ran while one was open for 7% of the time, Pallas kernels for 0%

profile of v1, /device:TPU:0, one launch (start us, length us, event | category | flops | bytes accessed | tf_op | source)
XLA Modules:
  0.0 156.3 jit_solution(1828819601898236460)
XLA Ops:
  0.0 3.0 %collective-permute-start = (bf16[1,8,5,32,128]{4,3,2,1,0:T(8,128)(2,1)}, bf16[1,8,5,32,128]{4,3,2,1,0:T(8,128)(2,1)S(1)}, u32[]{:S(2)}, u32[]{:S(2)}) collective-permute-start(bf16[1,8,5,32,128]{4,3,2,1,0:T(8,128)(2,1)} %param.7), channel_id=1, source_target_pairs={{0,1},{1,2},{2,3},{3,0},{4,5},{5,6},{6,7},{7,4},{8,9},{9,10},{10,1... | collective-permute-start | bytes 983048 | tf_op jit(solution)/shard_map/ppermute | solution.py:39
  3.0 2.0 %collective-permute-start.1 = (bf16[1,8,5,32,128]{4,3,2,1,0:T(8,128)(2,1)}, bf16[1,8,5,32,128]{4,3,2,1,0:T(8,128)(2,1)S(1)}, u32[]{:S(2)}, u32[]{:S(2)}) collective-permute-start(bf16[1,8,5,32,128]{4,3,2,1,0:T(8,128)(2,1)} %param.7), channel_id=1, source_target_pairs={{0,3},{1,0},{2,1},{3,2},{4,7},{5,4},{6,5},{7,6},{8,11},{9,8},{10,9... | collective-permute-start | bytes 983048 | tf_op jit(solution)/shard_map/ppermute | solution.py:44
  5.1 8.8 %collective-permute-done = bf16[1,8,5,32,128]{4,3,2,1,0:T(8,128)(2,1)S(1)} collective-permute-done((bf16[1,8,5,32,128]{4,3,2,1,0:T(8,128)(2,1)}, bf16[1,8,5,32,128]{4,3,2,1,0:T(8,128)(2,1)S(1)}, u32[]{:S(2)}, u32[]{:S(2)}) %collective-permute-start) | collective-permute-done | bytes 327712 | tf_op jit(solution)/shard_map/ppermute | solution.py:39
  13.8 0.0 collective-permute-start.2
  13.8 0.3 broadcast_in_dim.28
  14.1 1.0 constant_dynamic-update-slice_fusion.8
  15.2 4.4 %collective-permute-done.1 = bf16[1,8,5,32,128]{4,3,2,1,0:T(8,128)(2,1)S(1)} collective-permute-done((bf16[1,8,5,32,128]{4,3,2,1,0:T(8,128)(2,1)}, bf16[1,8,5,32,128]{4,3,2,1,0:T(8,128)(2,1)S(1)}, u32[]{:S(2)}, u32[]{:S(2)}) %collective-permute-start.1) | collective-permute-done | bytes 327712 | tf_op jit(solution)/shard_map/ppermute | solution.py:44
  19.7 7.4 %collective-permute-done.2 = bf16[1,8,5,32,128]{4,3,2,1,0:T(8,128)(2,1)S(1)} collective-permute-done((bf16[1,8,5,32,128]{4,3,2,1,0:T(8,128)(2,1)S(1)}, bf16[1,8,5,32,128]{4,3,2,1,0:T(8,128)(2,1)S(1)}, u32[]{:S(2)}, u32[]{:S(2)}) %collective-permute-start.2) | collective-permute-done | bytes 327712 | tf_op jit(solution)/shard_map/ppermute | solution.py:39
  27.1 3.5 %collective-permute-start.3 = (bf16[1,8,5,128,128]{4,3,2,1,0:T(8,128)(2,1)S(1)}, bf16[1,8,5,128,128]{4,3,2,1,0:T(8,128)(2,1)S(1)}, u32[]{:S(2)}, u32[]{:S(2)}) collective-permute-start(bf16[1,8,5,128,128]{4,3,2,1,0:T(8,128)(2,1)S(1)} %constant_dynamic-update-slice_fusion.5), channel_id=1, source_target_pairs={{0,8},{4,12},{8,16},{12,20},{16,24},{20,28},{1,9},{5,13},{9,17},{1... | collective-permute-start | bytes 3932168 | tf_op jit(solution)/shard_map/ppermute | solution.py:14
  30.6 2.4 %collective-permute-start.4 = (bf16[1,8,5,128,128]{4,3,2,1,0:T(8,128)(2,1)S(1)}, bf16[1,8,5,128,128]{4,3,2,1,0:T(8,128)(2,1)}, u32[]{:S(2)}, u32[]{:S(2)}) collective-permute-start(bf16[1,8,5,128,128]{4,3,2,1,0:T(8,128)(2,1)S(1)} %constant_dynamic-update-slice_fusion.5), channel_id=1, source_target_pairs={{0,4},{4,8},{8,12},{12,16},{16,20},{20,24},{24,28},{1,5},{5,9},{9,... | collective-permute-start | bytes 3932168 | tf_op jit(solution)/shard_map/ppermute | solution.py:14
  33.0 0.7 subtract_add_fusion
  33.6 1.3 collective-permute-start.5
  34.9 0.1 compare_select_fusion
  35.0 0.1 reshape.71
  35.1 1.3 collective-permute-start.6
  36.4 0.1 fusion.17
  36.4 0.1 copy.7
  36.5 0.7 broadcast_compare_fusion
  37.2 0.1 copy.6
  37.3 0.1 broadcast_bitcast_fusion
  37.4 22.3 %collective-permute-done.3 = bf16[1,8,5,128,128]{4,3,2,1,0:T(8,128)(2,1)S(1)} collective-permute-done((bf16[1,8,5,128,128]{4,3,2,1,0:T(8,128)(2,1)S(1)}, bf16[1,8,5,128,128]{4,3,2,1,0:T(8,128)(2,1)S(1)}, u32[]{:S(2)}, u32[]{:S(2)}) %collective-permute-start.3) | collective-permute-done | bytes 1310752 | tf_op jit(solution)/shard_map/ppermute | solution.py:14
  59.7 1.1 constant_dynamic-update-slice_fusion.4
  60.9 0.0 collective-permute-done.4
  60.9 2.5 %constant_dynamic-update-slice_fusion.3 = bf16[5,8,5,128,128]{4,3,2,1,0:T(8,128)(2,1)} fusion(bf16[5,8,5,128,128]{4,3,2,1,0:T(8,128)(2,1)} %constant_dynamic-update-slice_fusion.4, bf16[1,8,5,128,128]{4,3,2,1,0:T(8,128)(2,1)} %collective-permute-done.4), kind=kLoop, calls=%fused_computation.24 | loop fusion | bytes 2621440
  63.4 1.1 constant_dynamic-update-slice_fusion.2
  64.6 0.0 collective-permute-done.5
  64.6 2.5 %constant_dynamic-update-slice_fusion.1 = bf16[5,8,5,128,128]{4,3,2,1,0:T(8,128)(2,1)} fusion(bf16[5,8,5,128,128]{4,3,2,1,0:T(8,128)(2,1)} %constant_dynamic-update-slice_fusion.2, bf16[1,8,5,128,128]{4,3,2,1,0:T(8,128)(2,1)} %collective-permute-done.5), kind=kLoop, calls=%fused_computation.22 | loop fusion | bytes 2621440
  67.1 47.6 %collective-permute-done.6 = bf16[1,8,5,128,128]{4,3,2,1,0:T(8,128)(2,1)} collective-permute-done((bf16[1,8,5,128,128]{4,3,2,1,0:T(8,128)(2,1)S(1)}, bf16[1,8,5,128,128]{4,3,2,1,0:T(8,128)(2,1)}, u32[]{:S(2)}, u32[]{:S(2)}) %collective-permute-start.6) | collective-permute-done | bytes 1310752 | tf_op jit(solution)/shard_map/ppermute | solution.py:14
  114.7 2.6 %constant_dynamic-update-slice_fusion = bf16[5,8,5,128,128]{4,3,2,1,0:T(8,128)(2,1)} fusion(bf16[5,8,5,128,128]{4,3,2,1,0:T(8,128)(2,1)} %constant_dynamic-update-slice_fusion.1, bf16[1,8,5,128,128]{4,3,2,1,0:T(8,128)(2,1)} %collective-permute-done.6), kind=kLoop, calls=%fused_computation.21 | loop fusion | bytes 2621440 | tf_op jit(solution)/shard_map/concatenate | solution.py:55
  117.2 10.0 %gather_fusion = bf16[12,8,5,128,128]{4,3,2,1,0:T(8,128)(2,1)} fusion(bf16[5,8,5,128,128]{4,3,2,1,0:T(8,128)(2,1)} %constant_dynamic-update-slice_fusion, s32[1024]{0:T(1024)S(1)} %pad_clamp_fusion), kind=kCustom, calls=%fused_computation | custom fusion | bytes 31457328 | tf_op jit(solution)/shard_map/jit(_take)/gather | solution.py:59
  127.3 8.3 %copy_select_fusion = bf16[4,3,8,5,128,128]{5,4,2,0,3,1:T(8,128)(2,1)S(1)} fusion(bf16[4,3,8,5,128,128]{5,4,3,2,1,0:T(8,128)(2,1)} %bitcast.39, pred[4,3]{0,1:T(4,128)(4,1)S(1)} %copy.7), kind=kLoop, calls=%fused_computation.1 | loop fusion | flops 7864320 | bytes 31457292 | tf_op jit(solution)/shard_map/jit(_take)/select_n | solution.py:59
  135.5 0.0 copy-start
  135.5 3.7 %slice_bitcast_fusion.8 = (bf16[4,8,128,128]{3,2,1,0:T(8,128)(2,1)S(1)}, bf16[4,8,128,128]{3,2,1,0:T(8,128)(2,1)S(1)}, bf16[4,8,128,128]{3,2,1,0:T(8,128)(2,1)S(...) fusion(bf16[4,3,8,5,128,128]{5,4,2,0,3,1:T(8,128)(2,1)S(1)} %co, ...), kind=kLoop, calls=%fused_computation.19 | loop fusion | bytes 18874368 | tf_op jit(solution)/shard_map/squeeze | solution.py:21
  139.3 0.0 copy-done
  139.3 8.3 %fusion.29 = bf16[4,8,384,384]{3,2,1,0:T(8,128)(2,1)} fusion(bf16[4,8,128,128]{3,2,1,0:T(8,128)(2,1)S(1)} %get-tuple-element.6, bf16[4,8,128,128]{3,2,1,0:T(8,128)(2,1)S(1)} %get-tuple-element.7, bf16[4,8,128,128]{3,2,1,0:T(8,128)(2,1)S(1)} %get-tuple-element.8, bf16[4,8,128,128]{3,2,1,0:T(8,128)(2,1)S(1)} %get-tuple-element.9, ...), kind=kOutput, calls=%fused_computation.4.clone.clone.clone.2 | convolution fusion | flops 3714711552 | bytes 20055552 | tf_op jit(solution)/shard_map/pqij,pjk->pqik/dot_general | solution.py:64
  147.6 8.7 %and_select_fusion = f32[4,384,384]{2,1,0:T(8,128)} fusion(bf16[4,8,128,128]{3,2,1,0:T(8,128)(2,1)S(1)} %get-tuple-element.6, bf16[4,8,128,128]{3,2,1,0:T(8,128)(2,1)S(1)} %get-tuple-element.7, bf16[4,8,128,128]{3,2,1,0:T(8,128)(2,1)S(1)} %get-tuple-element.8, bf16[4,8,128,128]{3,2,1,0:T(8,128)(2,1)S(1)} %get-tuple-element.9, ...), kind=kOutput, calls=%fused_computation.6 | convolution fusion | flops 3709992960 | bytes 21235200 | tf_op jit(solution)/shard_map/pqik,pqlk->pil/dot_general | solution.py:67
  (4 shorter events, 0.1 us)
Async XLA Ops:
  0.0 13.8 %collective-permute-start = (bf16[1,8,5,32,128]{4,3,2,1,0:T(8,128)(2,1)}, bf16[1,8,5,32,128]{4,3,2,1,0:T(8,128)(2,1)S(1)}, u32[]{:S(2)}, u32[]{:S(2)}) collective-permute-start(bf16[1,8,5,32,128]{4,3,2,1,0:T(8,128)(2,1)} %param.7), channel_id=1, source_target_pairs={{0,1},{1,2},{2,3},{3,0},{4,5},{5,6},{6,7},{7,4},{8,9},{9,10},{10,1... | collective-permute-start | bytes 983048 | tf_op jit(solution)/shard_map/ppermute | solution.py:39
  3.0 16.6 %collective-permute-start.1 = (bf16[1,8,5,32,128]{4,3,2,1,0:T(8,128)(2,1)}, bf16[1,8,5,32,128]{4,3,2,1,0:T(8,128)(2,1)S(1)}, u32[]{:S(2)}, u32[]{:S(2)}) collective-permute-start(bf16[1,8,5,32,128]{4,3,2,1,0:T(8,128)(2,1)} %param.7), channel_id=1, source_target_pairs={{0,3},{1,0},{2,1},{3,2},{4,7},{5,4},{6,5},{7,6},{8,11},{9,8},{10,9... | collective-permute-start | bytes 983048 | tf_op jit(solution)/shard_map/ppermute | solution.py:44
  13.8 13.2 %collective-permute-start.2 = (bf16[1,8,5,32,128]{4,3,2,1,0:T(8,128)(2,1)S(1)}, bf16[1,8,5,32,128]{4,3,2,1,0:T(8,128)(2,1)S(1)}, u32[]{:S(2)}, u32[]{:S(2)}) collective-permute-start(bf16[1,8,5,32,128]{4,3,2,1,0:T(8,128)(2,1)S(1)} %collective-permute-done), channel_id=1, source_target_pairs={{0,1},{1,2},{2,3},{3,0},{4,5},{5,6},{6,7},{7,4},{8,9},{9,10},{10,1... | collective-permute-start | bytes 983048 | tf_op jit(solution)/shard_map/ppermute | solution.py:39
  27.1 32.6 %collective-permute-start.3 = (bf16[1,8,5,128,128]{4,3,2,1,0:T(8,128)(2,1)S(1)}, bf16[1,8,5,128,128]{4,3,2,1,0:T(8,128)(2,1)S(1)}, u32[]{:S(2)}, u32[]{:S(2)}) collective-permute-start(bf16[1,8,5,128,128]{4,3,2,1,0:T(8,128)(2,1)S(1)} %constant_dynamic-update-slice_fusion.5), channel_id=1, source_target_pairs={{0,8},{4,12},{8,16},{12,20},{16,24},{20,28},{1,9},{5,13},{9,17},{1... | collective-permute-start | bytes 3932168 | tf_op jit(solution)/shard_map/ppermute | solution.py:14
  30.6 30.3 %collective-permute-start.4 = (bf16[1,8,5,128,128]{4,3,2,1,0:T(8,128)(2,1)S(1)}, bf16[1,8,5,128,128]{4,3,2,1,0:T(8,128)(2,1)}, u32[]{:S(2)}, u32[]{:S(2)}) collective-permute-start(bf16[1,8,5,128,128]{4,3,2,1,0:T(8,128)(2,1)S(1)} %constant_dynamic-update-slice_fusion.5), channel_id=1, source_target_pairs={{0,4},{4,8},{8,12},{12,16},{16,20},{20,24},{24,28},{1,5},{5,9},{9,... | collective-permute-start | bytes 3932168 | tf_op jit(solution)/shard_map/ppermute | solution.py:14
  33.6 30.9 %collective-permute-start.5 = (bf16[1,8,5,128,128]{4,3,2,1,0:T(8,128)(2,1)S(1)}, bf16[1,8,5,128,128]{4,3,2,1,0:T(8,128)(2,1)}, u32[]{:S(2)}, u32[]{:S(2)}) collective-permute-start(bf16[1,8,5,128,128]{4,3,2,1,0:T(8,128)(2,1)S(1)} %constant_dynamic-update-slice_fusion.5), channel_id=1, source_target_pairs={{4,0},{8,4},{12,8},{16,12},{20,16},{24,20},{28,24},{5,1},{9,5},{13... | collective-permute-start | bytes 3932168 | tf_op jit(solution)/shard_map/ppermute | solution.py:14
  35.1 79.6 %collective-permute-start.6 = (bf16[1,8,5,128,128]{4,3,2,1,0:T(8,128)(2,1)S(1)}, bf16[1,8,5,128,128]{4,3,2,1,0:T(8,128)(2,1)}, u32[]{:S(2)}, u32[]{:S(2)}) collective-permute-start(bf16[1,8,5,128,128]{4,3,2,1,0:T(8,128)(2,1)S(1)} %constant_dynamic-update-slice_fusion.5), channel_id=1, source_target_pairs={{8,0},{12,4},{16,8},{20,12},{24,16},{28,20},{9,1},{13,5},{17,9},{2... | collective-permute-start | bytes 3932168 | tf_op jit(solution)/shard_map/ppermute | solution.py:14
  135.5 3.8 %copy-start = (bf16[4,384,384]{2,1,0:T(8,128)(2,1)S(1)}, bf16[4,384,384]{2,1,0:T(8,128)(2,1)}, u32[]{:S(2)}) copy-start(bf16[4,384,384]{2,1,0:T(8,128)(2,1)} %param.4) | copy-start | bytes 3538948
